TPU v7x, 32 devices: a whole 2x2x4 slice. The times are simulated.
32 devices in a mesh: ctx: 4 (over y, x), tp: 4 (over z), grp: 2 (over core).
Axes of the slice: x: 2, y: 2, z: 4, core: 2. Of those that a mesh axis runs over, the one named last changes fastest.
Arguments:
- patches: bfloat16 [32, 5120], P('ctx'), may hold values from -6 to 6
- route_count: int32 [4, 4], replicated, may hold values from 0 to 2, as said below
- text_states: bfloat16 [512, 4096], P('ctx', ('tp', 'grp')), may hold values from -6 to 6
- segment_ids: int32 [512], replicated, may hold values from 0 to 3, never falling along the last dimension, each value on 1 to 256 neighbouring positions
- vision_gain: float32 [1280], replicated, may hold values from 0.1 to 1.9
- merge_up: bfloat16 [5120, 2560], P(None, ('tp', 'grp')), may hold values from -0.078125 to 0.078125
- merge_down: bfloat16 [2560, 4096], P(('tp', 'grp')), may hold values from -0.125 to 0.125
- norm_gain: float32 [4096], replicated, may hold values from 0.1 to 1.9
- query_weight: bfloat16 [4096, 4096], P(None, ('tp', 'grp')), may hold values from -0.62928387 to 0.62928387
- kv_weight: bfloat16 [4096, 2048], P(None, 'tp'), may hold values from -0.4578688 to 0.4578688
Outputs:
- attended: bfloat16 [512, 4096], P('ctx', ('tp', 'grp'))
Inputs may be any that keep to these rules, and one draw needn't show every extreme that they name: route_count[c, d] counts the live rows among the 2 rows that source c holds for owner d; at least one owner gets 2 live rows from every source. `segment_ids`: never falling along the packed batch; a segment has at most 256 positions.
All inputs are finite; a program needn't handle non-finite values.
Results may differ from a plain program's by a relative error of at most 0.04.
Values may be sent and summed in bfloat16 or wider, within the bound.
A program may use at most 64 MiB of HBM per device.

v0:
```python
import jax
import jax.numpy as jnp
from jax import lax
from jax.sharding import PartitionSpec as P

HQ = 32
KVH = 8
HD = 128


EPSILON = 1e-06
NEGATIVE = -1e30


def rms_scale(values, gain):
    mean_square = jnp.mean(values * values, axis=-1, keepdims=True)
    return values * lax.rsqrt(mean_square + EPSILON) * gain


def attend(
    running,
    queries4,
    shard_piece,
    key_pos,
    query_pos,
    query_seg,
    segment_ids,
    visual_count,
    tokens_dev,
):
    weighted, running_max, denominator = running
    piece_rows = shard_piece.shape[0]
    kv_heads = queries4.shape[1]
    kv_split = shard_piece.reshape(piece_rows, kv_heads, 2, HD)
    key_block = kv_split[:, :, 0]
    value_block = kv_split[:, :, 1]
    key_owner = key_pos // tokens_dev
    owner_match = key_owner[:, None] == jnp.arange(visual_count.shape[0], dtype=jnp.int32)[None, :]
    visual_limit = jnp.sum(jnp.where(owner_match, visual_count[None, :], 0), axis=1)
    key_visual = key_pos % tokens_dev < visual_limit
    key_seg = segment_ids[key_pos]
    allowed = (query_seg[:, None] == key_seg[None, :]) & (
        key_visual[None, :] | (key_pos[None, :] <= query_pos[:, None])
    )
    scores = jnp.where(
        allowed,
        jnp.einsum("qkgd,rkd->kgqr", queries4, key_block, preferred_element_type=jnp.float32)
        * HD ** (-0.5),
        NEGATIVE,
    )
    new_max = jnp.maximum(running_max, jnp.max(scores, axis=-1))
    weights = jnp.exp(jnp.where(allowed, scores - new_max[..., None], NEGATIVE))
    denominator = jnp.sum(weights, axis=-1)
    weighted = jnp.einsum(
        "kgqr,rkd->kgqd",
        weights.astype(jnp.bfloat16),
        value_block,
        preferred_element_type=jnp.float32,
    )
    return (weighted, new_max, denominator)


def start_state(kv_heads, per_head, tokens_dev):
    return (
        jnp.zeros((kv_heads, per_head, tokens_dev, HD), jnp.float32),
        jnp.full((kv_heads, per_head, tokens_dev), NEGATIVE, jnp.float32),
        jnp.zeros((kv_heads, per_head, tokens_dev), jnp.float32),
    )


def shards(
    patches,
    route_count,
    text_states,
    segment_ids,
    vision_gain,
    merge_up,
    merge_down,
    norm_gain,
    query_weight,
    kv_weight,
):
    ctx_size = lax.axis_size("ctx")
    grp_size = lax.axis_size("grp")
    tp_size = lax.axis_size("tp")
    owner_index = lax.axis_index("ctx")
    member = lax.axis_index("grp")
    tp_index = lax.axis_index("tp")
    tensor_index = tp_index * grp_size + member
    row_count = patches.shape[0]
    bucket_rows = row_count // ctx_size
    tokens_dev = text_states.shape[0]
    grouped = patches.astype(jnp.float32).reshape(row_count, 4, -1)
    patch_normed = rms_scale(grouped, vision_gain).reshape(row_count, -1).astype(jnp.bfloat16)
    hidden = jax.nn.gelu(
        jnp.dot(patch_normed, merge_up, preferred_element_type=jnp.float32), approximate=False
    ).astype(jnp.bfloat16)
    partial_value = jnp.dot(hidden, merge_down, preferred_element_type=jnp.float32)
    column = lax.dynamic_slice_in_dim(route_count, owner_index, 1, 1)[:, 0]
    count_ends = jnp.cumsum(column)
    count_starts = count_ends - column
    slot_ids = jnp.arange(tokens_dev, dtype=jnp.int32)
    source = jnp.sum((count_ends[None, :] <= slot_ids[:, None]).astype(jnp.int32), axis=1)
    source = jnp.minimum(source, ctx_size - 1)
    source_match = source[:, None] == jnp.arange(ctx_size, dtype=jnp.int32)[None, :]
    first_slot = jnp.sum(jnp.where(source_match, count_starts[None, :], 0), axis=1)
    visual = slot_ids < count_ends[ctx_size - 1]
    pick_rows = jnp.where(visual, source * bucket_rows + slot_ids - first_slot, 0)
    merged = lax.psum(partial_value, ("tp", "grp")).astype(jnp.bfloat16)
    arrived = lax.all_to_all(
        merged.reshape(ctx_size, bucket_rows, -1), "ctx", split_axis=0, concat_axis=0, tiled=True
    )
    arrived = arrived.reshape(row_count, -1)
    text_full = lax.all_gather(text_states, ("tp", "grp"), axis=1, tiled=True)
    packed = jnp.where(visual[:, None], arrived[pick_rows], text_full)
    normal = rms_scale(packed.astype(jnp.float32), norm_gain).astype(jnp.bfloat16)
    queries = jnp.dot(normal, query_weight, preferred_element_type=jnp.float32).astype(jnp.bfloat16)
    kv_pairs = jnp.dot(normal, kv_weight, preferred_element_type=jnp.float32).astype(jnp.bfloat16)
    heads_dev = queries.shape[1] // HD
    group = HQ // KVH
    kv_per_tp = KVH // tp_size
    query_pos = owner_index * tokens_dev + slot_ids
    query_seg = segment_ids[query_pos]
    visual_count = jnp.sum(route_count, axis=0)
    kv_local = tensor_index * heads_dev // group - tp_index * kv_per_tp
    chosen = lax.dynamic_slice_in_dim(kv_pairs, kv_local * 2 * HD, 2 * HD, 1)
    queries4 = queries.reshape(tokens_dev, 1, heads_dev, HD)
    shard_piece = lax.all_gather(chosen, "ctx", axis=0, tiled=True)
    key_pos = jnp.arange(shard_piece.shape[0], dtype=jnp.int32)
    weighted, running_max, denominator = attend(
        start_state(1, heads_dev, tokens_dev),
        queries4,
        shard_piece,
        key_pos,
        query_pos,
        query_seg,
        segment_ids,
        visual_count,
        tokens_dev,
    )
    result = (weighted / denominator[..., None]).reshape(heads_dev, tokens_dev, HD)
    return result.transpose(1, 0, 2).reshape(tokens_dev, -1).astype(jnp.bfloat16)


def solution(mesh):
    return jax.shard_map(
        shards,
        mesh=mesh,
        in_specs=(
            P("ctx", None),
            P(),
            P("ctx", ("tp", "grp")),
            P(),
            P(),
            P(None, ("tp", "grp")),
            P(("tp", "grp"), None),
            P(),
            P(None, ("tp", "grp")),
            P(None, "tp"),
        ),
        out_specs=P("ctx", ("tp", "grp")),
        check_vma=False,
    )
```

profile of v0, /device:TPU:0, one launch (start us, length us, event | category | flops | bytes accessed | tf_op | source)
XLA Modules:
  0.0 106.3 jit_solution(12033060647353405200)
XLA Ops:
  6.5 0.0 copy-start
  6.5 1.0 convert_multiply_fusion.3
  7.6 0.1 reduce_sum.67
  7.7 0.7 mul.112
  8.4 0.1 mul.109
  8.5 0.0 copy-done
  8.5 0.0 copy-start.5
  8.5 0.0 copy-start.1
  8.5 4.6 %fusion.41 = f32[8,4096]{1,0:T(8,128)} fusion(bf16[320,4096]{1,0:T(8,128)(2,1)} %param.16, bf16[5120,320]{0,1:T(8,128)(2,1)S(1)} %copy-done, f32[8,5120]{1,0:T(8,128)S(1)} %bitcast.59, bf16[8,5120]{1,0:T(8,128)(2,1)} %param.10, f32[5120]{0:T(1024)S(1)} %mul.113), kind=kOutput, calls=%fused_computation.58 | convolution fusion | flops 47516160 | bytes 6295552 | tf_op jit(solution)/shard_map/dot_general | solution.py:98
  13.1 32.0 %all-reduce.1 = bf16[8,4096]{1,0:T(8,128)(2,1)S(1)} all-reduce(f32[8,4096]{1,0:T(8,128)} %fusion.41), channel_id=1, replica_groups=mesh['ctx'=4,'tp'=4,'grp'=2] {'tp','grp'}, use_global_device_ids=true, to_apply=%region_4.5 | all-reduce | flops 32768 | bytes 196608 | tf_op jit(solution)/shard_map/psum | solution.py:109
  45.2 0.7 reshape.183
  45.8 3.7 %all-to-all-start = ((bf16[4,2,4096]{2,1,0:T(2,128)(2,1)}), bf16[4,2,4096]{2,1,0:T(2,128)(2,1)S(1)}, u32[]{:S(2)}, u32[]{:S(2)}) async-start(bf16[4,2,4096]{2,1,0:T(2,128)(2,1)} %reshape.183), calls=%async_computation | async-start | bytes 131072 | tf_op jit(solution)/shard_map/all_to_all | solution.py:110
  49.6 0.0 all-gather.2.cloned.1.call-start
  49.6 0.7 all-gather.2.cloned.1.call-update
  50.3 0.0 copy-done.5
  50.3 0.2 fusion.112
  50.6 0.1 reduce.2
  50.7 0.6 slice.10
  51.3 0.0 copy-done.1
  51.3 1.3 %gather_fusion = s32[128]{0:T(128)S(1)} fusion(s32[512]{0:T(512)S(1)} %copy-done.1, s32[1024]{0:T(1024)S(1)} %pad_clamp_fusion.1), kind=kCustom, calls=%fused_computation | custom fusion | bytes 1536 | tf_op jit(solution)/shard_map/gather | solution.py:123
  52.6 3.5 %gather_fusion.1 = s32[512]{0:T(512)S(1)} fusion(s32[512]{0:T(512)S(1)} %copy-done.1, s32[1024]{0:T(1024)S(1)} %pad_clamp_fusion), kind=kCustom, calls=%fused_computation.1 | custom fusion | bytes 6144 | tf_op jit(solution)/shard_map/gather | solution.py:41
  56.1 0.1 convert_reduce_fusion
  56.2 0.1 select_reduce_fusion.1
  56.3 0.7 fusion.80
  57.0 0.1 select_reduce_fusion
  57.1 0.8 fusion.19
  57.9 0.7 iota_compare_fusion.4
  58.7 0.0 all-to-all-done
  58.7 2.2 %gather_fusion.2 = bf16[128,4096]{1,0:T(8,128)(2,1)} fusion(bf16[8,4096]{1,0:T(8,128)(2,1)S(1)} %reshape.184, s32[1024]{0:T(1024)S(1)} %pad_clamp_fusion.2), kind=kCustom, calls=%fused_computation.2 | custom fusion | bytes 2097664 | tf_op jit(solution)/shard_map/gather | solution.py:115
  60.9 0.0 copy-start.6
  60.9 12.1 %all-gather.2.cloned.1.call-done = bf16[128,4096]{1,0:T(8,128)(2,1)} async-done(((bf16[128,512]{1,0:T(8,128)(2,1)}), bf16[128,4096]{1,0:T(8,128)(2,1)}) %all-gather.2.cloned.1.call-update) | async-done | bytes 1048592 | tf_op jit(solution)/shard_map/all_gather | solution.py:114
  73.0 2.2 %fusion = (f32[128]{0:T(128)S(1)}, bf16[128,4096]{1,0:T(8,128)(2,1)S(1)}) fusion(bf16[128,4096]{1,0:T(8,128)(2,1)} %gather_fusion.2, bf16[128,4096]{1,0:T(8,128)(2,1)} %all-gather.2.cloned.1.call-done, pred[128]{0:T(512)(128)(4,1)S(1)} %iota_compare_fusion.4), kind=kLoop, calls=%fused_computation.5 | loop fusion | flops 2097024 | bytes 3146368 | tf_op jit(solution)/shard_map/reduce_sum | solution.py:16
  75.2 0.0 copy-start.2
  75.2 0.0 copy-start.7
  75.2 0.0 copy-done.6
  75.2 3.3 %fusion.16 = bf16[128,512]{1,0:T(8,128)(2,1)S(1)} fusion(bf16[4096,512]{1,0:T(8,128)(2,1)} %param.19, bf16[128,4096]{1,0:T(8,128)(2,1)S(1)} %get-tuple-element.6, f32[4096]{0:T(1024)S(1)} %copy-done.6, f32[128]{0:T(128)S(1)} %add_rsqrt_fusion.1), kind=kOutput, calls=%fused_computation.24 | convolution fusion | flops 538968064 | bytes 5390848 | tf_op jit(solution)/shard_map/dot_general | solution.py:118
  78.6 0.0 copy-done.2
  78.6 0.0 copy-done.7
  78.6 9.6 %all_gather.7 = bf16[512,256]{1,0:T(8,128)(2,1)} all-gather(bf16[128,256]{1,0:T(8,128)(2,1)S(1)} %dynamic-slice_convert_fusion), channel_id=1, replica_groups=mesh['ctx'=4,'tp'=4,'grp'=2] {'ctx'}, dimensions={0}, use_global_device_ids=true | all-gather | bytes 327680 | tf_op jit(solution)/shard_map/all_gather | solution.py:128
  88.2 1.0 reshape.185
  89.2 1.1 %fusion.113 = (bf16[512,1,1,128]{3,2,0,1:T(2,128)(2,1)}, bf16[512,1,1,128]{3,2,0,1:T(2,128)(2,1)S(1)}) fusion(bf16[512,1,2,128]{3,2,0,1:T(2,128)(2,1)S(1)} %reshape.185), kind=kLoop, calls=%fused_computation.155 | loop fusion | bytes 524288 | tf_op jit(solution)/shard_map/slice | solution.py:36
  90.3 0.0 copy-start.4
  90.3 0.0 copy-start.3
  90.3 3.3 %fusion.7 = bf16[16,4,8,128]{3,2,1,0:T(8,128)(2,1)S(1)} fusion(bf16[4096,512]{1,0:T(8,128)(2,1)} %param.18, bf16[128,4096]{1,0:T(8,128)(2,1)} %copy-done.2, f32[4096]{0:T(1024)S(1)} %copy-done.6, f32[128]{0:T(128)} %copy-done.7), kind=kOutput, calls=%fused_computation.15 | convolution fusion | flops 539033600 | bytes 5390848 | tf_op jit(solution)/shard_map/dot_general | solution.py:117
  93.6 0.0 copy-done.4
  93.6 1.3 %fusion.114 = (f32[4,128]{1,0:T(4,128)S(1)}, f32[1,4,128,512]{2,3,1,0:T(8,128)}) fusion(bf16[16,4,8,128]{3,2,1,0:T(8,128)(2,1)S(1)} %fusion.7, bf16[512,1,1,128]{3,2,0,1:T(2,128)(2,1)S(1)} %get-tuple-element.10, pred[128,512]{0,1:T(8,128)(4,1)S(1)} %copy-done.4), kind=kOutput, calls=%fused_computation.156 | convolution fusion | flops 67894784 | bytes 1378304 | tf_op jit(solution)/shard_map/qkgd,rkd->kgqr/dot_general | solution.py:47
  94.9 0.0 copy-done.3
  94.9 0.8 copy.27
  95.7 1.4 %fusion.8 = f32[4,128]{1,0:T(4,128)S(1)} fusion(f32[1,4,128,512]{2,3,1,0:T(8,128)} %get-tuple-element.12, f32[4,128]{1,0:T(4,128)S(1)} %broadcast_maximum_fusion, pred[128,512]{0,1:T(8,128)(4,1)} %fusion.19), kind=kLoop, calls=%fused_computation.18 | loop fusion | flops 785920 | bytes 1118208 | tf_op jit(solution)/shard_map/reduce_sum | solution.py:53
  97.1 1.6 %fusion.6 = bf16[128,4,128]{0,2,1:T(8,128)(2,1)S(1)} fusion(f32[1,4,128,512]{2,3,1,0:T(8,128)} %get-tuple-element.12, f32[4,128]{1,0:T(4,128)S(1)} %broadcast_maximum_fusion, pred[128,512]{0,1:T(8,128)(4,1)} %fusion.19, bf16[512,1,1,128]{0,3,2,1:T(8,128)(2,1)} %copy.27, f32[128,4]{0,1:T(4,128)S(1)} %bitcast.62), kind=kOutput, calls=%fused_computation.13 | convolution fusion | flops 68026368 | bytes 1380352 | tf_op jit(solution)/shard_map/kgqr,rkd->kgqd/dot_general | solution.py:54
  98.7 0.8 copy.25
  (18 shorter events, 0.2 us)
Async XLA Ops:
  6.5 2.0 %copy-start = (bf16[5120,320]{0,1:T(8,128)(2,1)S(1)}, bf16[5120,320]{0,1:T(8,128)(2,1)}, u32[]{:S(2)}) copy-start(bf16[5120,320]{0,1:T(8,128)(2,1)} %param.15) | copy-start | bytes 9830404
  8.5 41.8 %copy-start.5 = (s32[4,4]{1,0:T(4,128)S(1)}, s32[4,4]{1,0:T(4,128)}, u32[]{:S(2)}) copy-start(s32[4,4]{1,0:T(4,128)} %param.11) | copy-start | bytes 196
  8.5 42.8 %copy-start.1 = (s32[512]{0:T(512)S(1)}, s32[512]{0:T(512)}, u32[]{:S(2)}) copy-start(s32[512]{0:T(512)} %param.13) | copy-start | bytes 6148
  45.8 12.8 %all-to-all-start = ((bf16[4,2,4096]{2,1,0:T(2,128)(2,1)}), bf16[4,2,4096]{2,1,0:T(2,128)(2,1)S(1)}, u32[]{:S(2)}, u32[]{:S(2)}) async-start(bf16[4,2,4096]{2,1,0:T(2,128)(2,1)} %reshape.183), calls=%async_computation | async-start | bytes 131072 | tf_op jit(solution)/shard_map/all_to_all | solution.py:110
  49.6 23.5 %all-gather.2.cloned.1.call-start = ((), (), s32[]{:S(2)}) async-start(), calls=%async_computation.1 | async-start | bytes 1179648 | tf_op jit(solution)/shard_map/all_gather | solution.py:114
  60.9 14.3 %copy-start.6 = (f32[4096]{0:T(1024)S(1)}, f32[4096]{0:T(1024)}, u32[]{:S(2)}) copy-start(f32[4096]{0:T(1024)} %param.17) | copy-start | bytes 49156
  75.2 3.4 %copy-start.2 = (bf16[128,4096]{1,0:T(8,128)(2,1)}, bf16[128,4096]{1,0:T(8,128)(2,1)S(1)}, u32[]{:S(2)}) copy-start(bf16[128,4096]{1,0:T(8,128)(2,1)S(1)} %get-tuple-element.6) | copy-start | bytes 3145732
  75.2 3.4 %copy-start.7 = (f32[128]{0:T(128)}, f32[128]{0:T(128)S(1)}, u32[]{:S(2)}) copy-start(f32[128]{0:T(128)S(1)} %add_rsqrt_fusion.1) | copy-start | bytes 1540
  90.3 3.3 %copy-start.4 = (pred[128,512]{0,1:T(8,128)(4,1)S(1)}, pred[128,512]{0,1:T(8,128)(4,1)}, u32[]{:S(2)}) copy-start(pred[128,512]{0,1:T(8,128)(4,1)} %fusion.19) | copy-start | bytes 196612
  90.3 4.6 %copy-start.3 = (bf16[512,1,1,128]{3,2,0,1:T(2,128)(2,1)S(1)}, bf16[512,1,1,128]{3,2,0,1:T(2,128)(2,1)}, u32[]{:S(2)}) copy-start(bf16[512,1,1,128]{3,2,0,1:T(2,128)(2,1)} %get-tuple-element.9) | copy-start | bytes 393220
Sparse Core Ops, SparseCore 0:
  52.0 21.0 all-gather.1
where the time goes:
time: 107 us; the launch traced here: 106 us
  blocking collectives  41.6 us (39%)
  matrix products  14.1 us (13%)
  between operations  13.7 us (13%)
  local copies, waits for them, and re-layouts  13 us (12%)
  waiting for transfers between devices  12.8 us (12%)
  other arithmetic  7.46 us (7%)
  starting transfers between devices  3.72 us (3%)
    psum x1, blocking collectives, shards(): merged = lax.psum(partial_value, ('tp', 'grp')).astype(jnp.bfloat16)  32 us
    all_gather x1, waiting for transfers between devices, shards(): text_full = lax.all_gather(text_states, ('tp', 'grp'), axis=1, tiled=True)  12.1 us
    all_gather x1, blocking collectives, shards(): shard_piece = lax.all_gather(chosen, 'ctx', axis=0, tiled=True)  9.55 us
    dot_general x1, matrix products, shards(): jnp.dot(hidden, merge_down, preferred_element_type=jnp.float32)  4.57 us
    all_to_all x1, starting transfers between devices, shards(): lax.all_to_all(merged.reshape(ctx_size, bucket_rows, -1), 'ctx', split_ax...  3.72 us
    gather x1, local copies, waits for them, and re-layouts, attend(): key_seg = segment_ids[key_pos]  3.49 us
    dot_general x1, matrix products, shards(): jnp.dot(normal, kv_weight, preferred_element_type=jnp.float32)  3.34 us
    dot_general x1, matrix products, shards(): jnp.dot(normal, query_weight, preferred_element_type=jnp.float32)  3.32 us
  transfers between devices with their start and end apart: 2, of which 1 were waited for; matrix products, arithmetic and copies ran while one was open for 10% of the time, Pallas kernels for 0%

commit v1 on v0

--- a/solution.py
+++ b/solution.py
@@ -1,6 +1,10 @@
+import functools
+
 import jax
 import jax.numpy as jnp
 from jax import lax
+from jax.experimental import pallas as pl
+from jax.experimental.pallas import tpu as pltpu
 from jax.sharding import PartitionSpec as P
 
 HQ = 32
@@ -68,7 +72,7 @@
     )
 
 
-def shards(
+def shards_wide(
     patches,
     route_count,
     text_states,
@@ -142,9 +146,489 @@
     return result.transpose(1, 0, 2).reshape(tokens_dev, -1).astype(jnp.bfloat16)
 
 
+MESH = pl.DeviceIdType.MESH
+UP_CHUNKS = 4
+BF16 = jnp.bfloat16
+F32 = jnp.float32
+
+
+def fits(mesh):
+    return mesh.shape["grp"] == 2 and mesh.size <= 64
+
+
+def erf(value):
+    value = jnp.clip(value, -4.0, 4.0)
+    square = value * value
+    top = jnp.full_like(value, -2.72614225801306e-10)
+    for factor in (
+        2.77068142495902e-08,
+        -2.10102402082508e-06,
+        -5.69250639462346e-05,
+        -7.34990630326855e-04,
+        -2.95459980854025e-03,
+        -1.60960333262415e-02,
+    ):
+        top = top * square + factor
+    low = jnp.full_like(value, -1.45660718464996e-05)
+    for factor in (
+        -2.13374055278905e-04,
+        -1.68282697438203e-03,
+        -7.37332916720468e-03,
+        -1.42647390514189e-02,
+    ):
+        low = low * square + factor
+    return value * top / low
+
+
+def remote(src, dst, send, recv, where):
+    return pltpu.make_async_remote_copy(
+        src_ref=src,
+        dst_ref=dst,
+        send_sem=send,
+        recv_sem=recv,
+        device_id=where,
+        device_id_type=MESH,
+    )
+
+
+def body(
+    ctx_size,
+    tp_size,
+    grp_size,
+    kv_heads_tp,
+    patches,
+    route,
+    text,
+    seg,
+    vgain,
+    up,
+    down,
+    ngain,
+    wq,
+    wkv,
+    out,
+    up_v,
+    down_v,
+    wq_v,
+    wkv_v,
+    full,
+    rs_send,
+    rs_recv,
+    merged,
+    arrived,
+    gathered,
+    vis,
+    normal,
+    queries,
+    kv_full,
+    load_sem,
+    own_sem,
+    text_recv,
+    up_send,
+    down_send,
+    side_send,
+    rs_send_sem,
+    rs_recv_sem,
+    row_send,
+    row_recv,
+    row_own,
+    vis_send,
+    vis_recv,
+    vis_own,
+    kv_send,
+    kv_recv,
+):
+    c = lax.axis_index("ctx")
+    z = lax.axis_index("tp")
+    g = lax.axis_index("grp")
+    members = tp_size * grp_size
+    mine = z * grp_size + g
+    rows, features_in = patches.shape
+    bucket = rows // ctx_size
+    tokens_dev, width = text.shape
+    heads_dev = wq.shape[1] // HD
+    group = HQ // KVH
+    vis_rows = ctx_size * bucket
+
+    part = features_in // UP_CHUNKS
+    up_loads = [
+        pltpu.make_async_copy(
+            up.at[pl.ds(i * part, part)], up_v.at[pl.ds(i * part, part)], load_sem.at[i]
+        )
+        for i in range(UP_CHUNKS)
+    ]
+    down_load = pltpu.make_async_copy(down, down_v, load_sem.at[UP_CHUNKS])
+    kv_local = mine * heads_dev // group - z * kv_heads_tp
+    kv_columns = pl.ds(pl.multiple_of(kv_local * 2 * HD, 2 * HD), 2 * HD)
+    kv_load = pltpu.make_async_copy(wkv.at[:, kv_columns], wkv_v, load_sem.at[UP_CHUNKS + 1])
+    q_load = pltpu.make_async_copy(wq, wq_v, load_sem.at[UP_CHUNKS + 2])
+    own_text = pltpu.make_async_copy(text, full.at[mine], own_sem)
+    own_text.start()
+    for load in up_loads:
+        load.start()
+    down_load.start()
+    kv_load.start()
+    q_load.start()
+
+    tensor_peers = []
+    for step in range(1, members):
+        other = lax.rem(mine + step, members)
+        tensor_peers.append((other, {"tp": other // grp_size, "grp": lax.rem(other, grp_size)}))
+    ctx_peers = []
+    for step in range(1, ctx_size):
+        other = lax.rem(c + step, ctx_size)
+        ctx_peers.append((other, {"ctx": other}))
+    barrier = pltpu.get_barrier_semaphore()
+    for _, where in tensor_peers + ctx_peers:
+        pl.semaphore_signal(barrier, inc=1, device_id=where, device_id_type=MESH)
+    pl.semaphore_wait(barrier, len(tensor_peers) + len(ctx_peers))
+
+    def up_copy(step):
+        slot = (z - step) * grp_size + g
+        src = text if step == 0 else full.at[slot]
+        return remote(src, full.at[slot], up_send.at[step], text_recv.at[slot], {"tp": z + 1})
+
+    def down_copy(step):
+        slot = (z + step) * grp_size + g
+        src = text if step == 0 else full.at[slot]
+        return remote(src, full.at[slot], down_send.at[step], text_recv.at[slot], {"tp": z - 1})
+
+    def side_copy(from_z, own):
+        slot = from_z * grp_size + g
+        src = text if own else full.at[slot]
+        return remote(src, full.at[slot], side_send.at[from_z], text_recv.at[slot], {"grp": 1 - g})
+
+    def slot_arrived(slot):
+        remote(
+            full.at[slot], full.at[slot], up_send.at[0], text_recv.at[slot], {"grp": 1 - g}
+        ).wait_recv()
+
+    def sends_up(step):
+        return (z >= step) & (z + 1 < tp_size)
+
+    def sends_down(step):
+        return (z + step < tp_size) & (z >= 1)
+
+    def text_step(step):
+        if step == 0:
+            side_now = [(z, None)]
+        else:
+            side_now = [(z - step, z >= step), (z + step, z + step < tp_size)]
+            for from_z, there in side_now:
+
+                @pl.when(there)
+                def _():
+                    slot_arrived(from_z * grp_size + g)
+
+        if step < tp_size - 1:
+
+            @pl.when(sends_up(step))
+            def _():
+                up_copy(step).start()
+
+            @pl.when(sends_down(step))
+            def _():
+                down_copy(step).start()
+
+        for from_z, there in side_now:
+            if there is None:
+                side_copy(from_z, True).start()
+            else:
+
+                @pl.when(there)
+                def _():
+                    side_copy(from_z, False).start()
+
+    text_step(0)
+
+    grouped = patches.shape[1] // vgain.shape[1]
+    span = vgain.shape[1]
+    normed = []
+    for i in range(grouped):
+        piece = patches[:, i * span : (i + 1) * span].astype(F32)
+        scale = lax.rsqrt(jnp.mean(piece * piece, axis=-1, keepdims=True) + EPSILON)
+        normed.append((piece * scale * vgain[...]).astype(BF16))
+    hidden = jnp.zeros((rows, up.shape[1]), F32)
+    for i in range(UP_CHUNKS):
+        up_loads[i].wait()
+        hidden = hidden + jnp.dot(
+            normed[i], up_v[i * part : (i + 1) * part, :], preferred_element_type=F32
+        )
+    hidden = (0.5 * hidden * (1.0 + erf(hidden * 0.5**0.5))).astype(BF16)
+    down_load.wait()
+    for t in range(members):
+        piece = jnp.dot(
+            hidden, down_v[:, t * width : (t + 1) * width], preferred_element_type=F32
+        )
+        rs_send[t] = piece.astype(rs_send.dtype)
+
+    rs_copies = []
+    for i, (other, where) in enumerate(tensor_peers):
+        copy = remote(
+            rs_send.at[other], rs_recv.at[mine], rs_send_sem.at[i], rs_recv_sem.at[mine], where
+        )
+        copy.start()
+        rs_copies.append(copy)
+    for step in range(1, tp_size - 1):
+        text_step(step)
+    total = rs_send[mine].astype(F32)
+    for i, (other, where) in enumerate(tensor_peers):
+        remote(
+            rs_send.at[other], rs_recv.at[other], rs_send_sem.at[i], rs_recv_sem.at[other], where
+        ).wait_recv()
+        total = total + rs_recv[other].astype(F32)
+    total = total.astype(BF16).astype(merged.dtype)
+    for d in range(ctx_size):
+        merged[d] = total[d * bucket : (d + 1) * bucket, :]
+
+    row_copies = []
+    for i, (other, where) in enumerate(ctx_peers):
+        copy = remote(
+            merged.at[other], arrived.at[c], row_send.at[i], row_recv.at[c], where
+        )
+        copy.start()
+        row_copies.append(copy)
+    row_keep = pltpu.make_async_copy(merged.at[c], arrived.at[c], row_own)
+    row_keep.start()
+    text_step(tp_size - 1)
+    row_keep.wait()
+    for i, (other, where) in enumerate(ctx_peers):
+        remote(
+            merged.at[other], arrived.at[other], row_send.at[i], row_recv.at[other], where
+        ).wait_recv()
+    vis_copies = []
+    for i, (other, where) in enumerate(tensor_peers):
+        copy = remote(arrived, gathered.at[mine], vis_send.at[i], vis_recv.at[mine], where)
+        copy.start()
+        vis_copies.append(copy)
+    vis_keep = pltpu.make_async_copy(arrived, gathered.at[mine], vis_own)
+    vis_keep.start()
+
+    own_text.wait()
+    for t in range(members):
+
+        @pl.when(t % grp_size != g)
+        def _():
+            slot_arrived(t)
+
+    squares = jnp.zeros((tokens_dev, 1), F32)
+    for t in range(members):
+        piece = full[t].astype(F32)
+        squares = squares + jnp.sum(piece * piece, axis=-1, keepdims=True)
+    features = members * width
+    scale = lax.rsqrt(squares / features + EPSILON)
+    for t in range(members):
+        gain = ngain[:, t * width : (t + 1) * width]
+        normal[:, t * width : (t + 1) * width] = (full[t].astype(F32) * scale * gain).astype(BF16)
+    kv_load.wait()
+    kv_full[c] = jnp.dot(normal[...], wkv_v[...], preferred_element_type=F32).astype(BF16)
+    late = -(-vis_rows // 16) * 16
+    tail = pl.ds(late, tokens_dev - late)
+    first = pl.ds(0, late)
+    kv_copies = []
+
+    def kv_copy(i, where, block, span_rows, phase):
+        return remote(
+            kv_full.at[block, span_rows],
+            kv_full.at[block, span_rows],
+            kv_send.at[phase, i],
+            kv_recv.at[phase, block],
+            where,
+        )
+
+    for i, (other, where) in enumerate(ctx_peers):
+        copy = kv_copy(i, where, c, tail, 0)
+        copy.start()
+        kv_copies.append(copy)
+    q_load.wait()
+    for n in range(0, queries.shape[1], 2 * HD):
+        queries[:, n : n + 2 * HD] = jnp.dot(
+            normal[...], wq_v[:, n : n + 2 * HD], preferred_element_type=F32
+        ).astype(BF16)
+
+    slot_of = lax.broadcasted_iota(jnp.int32, (late, vis_rows), 0)
+    row_of = lax.broadcasted_iota(jnp.int32, (late, vis_rows), 1)
+    chosen = jnp.zeros((late, vis_rows), F32)
+    start = jnp.int32(0)
+    for source in range(ctx_size):
+        count = route[source, c]
+        for j in range(bucket):
+            at = jnp.where(j < count, start + j, -1)
+            hit = (slot_of == at) & (row_of == source * bucket + j)
+            chosen = jnp.where(hit, 1.0, chosen)
+        start = start + count
+    chosen = chosen.astype(BF16)
+    is_visual = lax.broadcasted_iota(jnp.int32, (late, 1), 0) < start
+
+    vis_keep.wait()
+    for i, (other, where) in enumerate(tensor_peers):
+        remote(
+            arrived, gathered.at[other], vis_send.at[i], vis_recv.at[other], where
+        ).wait_recv()
+    for t in range(members):
+        for source in range(ctx_size):
+            vis[source * bucket : (source + 1) * bucket, t * width : (t + 1) * width] = gathered[
+                t, source
+            ].astype(F32)
+    visual = vis[...]
+    scale = lax.rsqrt(jnp.mean(visual * visual, axis=-1, keepdims=True) + EPSILON)
+    visual = (visual * scale * ngain[...]).astype(BF16)
+    visual = jnp.dot(chosen, visual, preferred_element_type=F32).astype(BF16)
+    kv_rows = jnp.dot(visual, wkv_v[...], preferred_element_type=F32).astype(BF16)
+    kv_full[c, 0:late, :] = jnp.where(
+        is_visual, kv_rows.astype(F32), kv_full[c, 0:late, :].astype(F32)
+    ).astype(BF16)
+    for i, (other, where) in enumerate(ctx_peers):
+        copy = kv_copy(i, where, c, first, 1)
+        copy.start()
+        kv_copies.append(copy)
+    for n in range(0, queries.shape[1], 2 * HD):
+        query_rows = jnp.dot(visual, wq_v[:, n : n + 2 * HD], preferred_element_type=F32)
+        queries[0:late, n : n + 2 * HD] = jnp.where(
+            is_visual,
+            query_rows.astype(BF16).astype(F32),
+            queries[0:late, n : n + 2 * HD].astype(F32),
+        ).astype(BF16)
+
+    mine_row = jnp.broadcast_to(seg[pl.ds(c, 1), :], (tokens_dev, tokens_dev))
+    query_seg = mine_row.T
+    lane = lax.broadcasted_iota(jnp.int32, (tokens_dev, tokens_dev), 1)
+    row = lax.broadcasted_iota(jnp.int32, (tokens_dev, tokens_dev), 0)
+    query_pos = c * tokens_dev + row
+    allowed = []
+    for block in range(ctx_size):
+        count = route[0, block]
+        for source in range(1, ctx_size):
+            count = count + route[source, block]
+        near = (lane < count) | (block * tokens_dev + lane <= query_pos)
+        allowed.append((query_seg == seg[block : block + 1, :]) & near)
+    bias = jnp.concatenate([jnp.where(ok, 0.0, NEGATIVE) for ok in allowed], axis=1)
+
+    for phase, span_rows in ((0, tail), (1, first)):
+        for i, (other, where) in enumerate(ctx_peers):
+            kv_copy(i, where, other, span_rows, phase).wait_recv()
+    keys = jnp.concatenate([kv_full[b, :, :HD] for b in range(ctx_size)], axis=0)
+    values = jnp.concatenate([kv_full[b, :, HD:] for b in range(ctx_size)], axis=0)
+    for h in range(heads_dev):
+        query = queries[:, h * HD : (h + 1) * HD]
+        scores = lax.dot_general(
+            query, keys, (((1,), (1,)), ((), ())), preferred_element_type=F32
+        )
+        scores = jnp.where(bias == 0.0, scores * HD ** (-0.5), NEGATIVE)
+        weights = jnp.exp(scores - jnp.max(scores, axis=-1, keepdims=True))
+        total = jnp.sum(weights, axis=-1, keepdims=True)
+        mixed = jnp.dot(weights.astype(BF16), values, preferred_element_type=F32)
+        out[:, h * HD : (h + 1) * HD] = (mixed / total).astype(BF16)
+
+    for step in range(tp_size - 1):
+
+        @pl.when(sends_up(step))
+        def _():
+            up_copy(step).wait_send()
+
+        @pl.when(sends_down(step))
+        def _():
+            down_copy(step).wait_send()
+
+    for from_z in range(tp_size):
+        side_copy(from_z, False).wait_send()
+    for copy in rs_copies + row_copies + vis_copies + kv_copies:
+        copy.wait_send()
+
+
+def fused(
+    patches,
+    route_count,
+    text_states,
+    segment_ids,
+    vision_gain,
+    merge_up,
+    merge_down,
+    norm_gain,
+    query_weight,
+    kv_weight,
+):
+    ctx_size = lax.axis_size("ctx")
+    tp_size = lax.axis_size("tp")
+    grp_size = lax.axis_size("grp")
+    members = tp_size * grp_size
+    rows = patches.shape[0]
+    bucket = rows // ctx_size
+    tokens_dev, width = text_states.shape
+    features = query_weight.shape[0]
+    vmem = pl.BlockSpec(memory_space=pltpu.VMEM)
+    anywhere = pl.BlockSpec(memory_space=pl.ANY)
+    scalars = pl.BlockSpec(memory_space=pltpu.SMEM)
+    dma = pltpu.SemaphoreType.DMA
+    kernel = functools.partial(body, ctx_size, tp_size, grp_size, KVH // tp_size)
+    return pl.pallas_call(
+        kernel,
+        out_shape=jax.ShapeDtypeStruct((tokens_dev, query_weight.shape[1]), BF16),
+        in_specs=[
+            vmem,
+            scalars,
+            anywhere,
+            vmem,
+            vmem,
+            anywhere,
+            anywhere,
+            vmem,
+            anywhere,
+            anywhere,
+        ],
+        out_specs=vmem,
+        scratch_shapes=[
+            pltpu.VMEM(merge_up.shape, BF16),
+            pltpu.VMEM(merge_down.shape, BF16),
+            pltpu.VMEM(query_weight.shape, BF16),
+            pltpu.VMEM((features, 2 * HD), BF16),
+            pltpu.VMEM((members, tokens_dev, width), BF16),
+            pltpu.VMEM((members, rows, width), BF16),
+            pltpu.VMEM((members, rows, width), BF16),
+            pltpu.VMEM((ctx_size, bucket, width), F32),
+            pltpu.VMEM((ctx_size, bucket, width), F32),
+            pltpu.VMEM((members, ctx_size, bucket, width), F32),
+            pltpu.VMEM((rows, features), F32),
+            pltpu.VMEM((tokens_dev, features), BF16),
+            pltpu.VMEM((tokens_dev, query_weight.shape[1]), BF16),
+            pltpu.VMEM((ctx_size, tokens_dev, 2 * HD), BF16),
+            dma((UP_CHUNKS + 3,)),
+            dma,
+            dma((members,)),
+            dma((tp_size,)),
+            dma((tp_size,)),
+            dma((tp_size,)),
+            dma((members,)),
+            dma((members,)),
+            dma((ctx_size,)),
+            dma((ctx_size,)),
+            dma,
+            dma((members,)),
+            dma((members,)),
+            dma,
+            dma((2, ctx_size)),
+            dma((2, ctx_size)),
+        ],
+        compiler_params=pltpu.CompilerParams(
+            collective_id=0, has_side_effects=True, vmem_limit_bytes=56 * 2**20
+        ),
+    )(
+        patches,
+        route_count,
+        text_states,
+        segment_ids.reshape(ctx_size, tokens_dev),
+        vision_gain.reshape(1, -1),
+        merge_up,
+        merge_down,
+        norm_gain.reshape(1, -1),
+        query_weight,
+        kv_weight,
+    )
+
+
 def solution(mesh):
     return jax.shard_map(
-        shards,
+        fused if fits(mesh) else shards_wide,
         mesh=mesh,
         in_specs=(
             P("ctx", None),

time: 107 us -> 39.8 us (0.37)
  blocking collectives: 41.6 us -> 0 us
  Pallas kernels: 0 us -> 30.8 us
  matrix products: 14.1 us -> 0 us
  between operations: 13.7 us -> 0.01 us
  waiting for transfers between devices: 12.8 us -> 0 us
  other arithmetic: 7.46 us -> 0 us
  local copies, waits for them, and re-layouts: 13 us -> 8.71 us
  starting transfers between devices: 3.72 us -> 0 us
    psum x1 -> x0, blocking collectives: 32 us -> none  [shards(): merged = lax.psum(partial_value, ('tp', 'grp')).astype(jnp.bfloat16)]
    pallas_call x0 -> x1, Pallas kernels: none -> 30.8 us  [fused(): pl.pallas_call(kernel, out_shape=jax.ShapeDtypeStruct((tokens_dev, query_...]
    dot_general x5 -> x0, matrix products: 14.1 us -> none  [the longest x1 4.57 us: shards(): jnp.dot(hidden, merge_down, preferred_element_type=jnp.float32)]
    all_gather x1 -> x0, waiting for transfers between devices: 12.1 us -> none  [shards(): text_full = lax.all_gather(text_states, ('tp', 'grp'), axis=1, tiled=True)]
    all_gather x1 -> x0, blocking collectives: 9.55 us -> none  [shards(): shard_piece = lax.all_gather(chosen, 'ctx', axis=0, tiled=True)]
    gather x3 -> x0, local copies, waits for them, and re-layouts: 6.99 us -> none  [the longest x1 3.49 us: attend(): key_seg = segment_ids[key_pos]]
    unnamed x17 -> x2, local copies, waits for them, and re-layouts: 0.82 us -> 7.41 us
    reduce_sum x7 -> x0, other arithmetic: 3.96 us -> none  [the longest x2 2.26 us: rms_scale(): mean_square = jnp.mean(values * values, axis=-1, keepdims=True)]
  transfers between devices with their start and end apart: 2 -> 0, of which waited for: 1 -> 0; matrix products, arithmetic and copies ran while one was open for 10% -> 0% of each run, Pallas kernels for 0% -> 0%
where the time goes in v1:
time: 39.8 us; the launch traced here: 39.5 us
  Pallas kernels  30.8 us (77%)
  local copies, waits for them, and re-layouts  8.71 us (22%)
    pallas_call x1, Pallas kernels, fused(): pl.pallas_call(kernel, out_shape=jax.ShapeDtypeStruct((tokens_dev, query_...  30.8 us
    unnamed x2, local copies, waits for them, and re-layouts  7.41 us
    reshape x1, local copies, waits for them, and re-layouts, fused(): vision_gain.reshape(1, -1)  1.29 us

profile of v1, /device:TPU:0, one launch (start us, length us, event | category | flops | bytes accessed | tf_op | source)
XLA Modules:
  0.0 39.5 jit_solution(10375627128484951986)
XLA Ops:
  0.0 1.3 %reshape.10.vgain = f32[1,1280]{1,0:T(1,128)} reshape(f32[1280]{0:T(1024)} %param.14) | data formatting | bytes 10240 | tf_op jit(solution)/shard_map/reshape | solution.py:620
  1.3 5.8 %copy.11.up = bf16[5120,320]{1,0:T(8,128)(2,1)} copy(bf16[5120,320]{0,1:T(8,128)(2,1)} %param.15) | data formatting | bytes 6553600 | tf_op args[5]
  7.1 30.8 %shard_map.100 = bf16[128,512]{1,0:T(8,128)(2,1)} custom-call(bf16[8,5120]{1,0:T(8,128)(2,1)} %patches.1, s32[4,4]{1,0:T(4,128)} %route.1, bf16[128,512]{1,0:T(8,128)(2,1)} %text.1, s32[4,128]{1,0:T(4,128)} %bitcast.3, f32[1,1280]{1,0:T(1,128)} %reshape.10.vgain, bf16[5120,320]{1,0:T(8,128)(2,1)} %copy.11.up, bf16[320,4096]{1,0:T(8,128)(2,1)} %down.1, ...), custom_call_target="tpu_custom_call" | custom-call | tf_op jit(solution)/shard_map/pallas_call | solution.py:564
  37.9 1.6 %copy.13 = bf16[128,512]{1,0:T(8,128)(2,1)} copy(bf16[128,512]{1,0:T(8,128)(2,1)} %shard_map.100) | data formatting | bytes 262144

commit v2 on v1

--- a/solution.py
+++ b/solution.py
@@ -147,7 +147,6 @@
 
 
 MESH = pl.DeviceIdType.MESH
-UP_CHUNKS = 4
 BF16 = jnp.bfloat16
 F32 = jnp.float32
 
@@ -250,26 +249,6 @@
     group = HQ // KVH
     vis_rows = ctx_size * bucket
 
-    part = features_in // UP_CHUNKS
-    up_loads = [
-        pltpu.make_async_copy(
-            up.at[pl.ds(i * part, part)], up_v.at[pl.ds(i * part, part)], load_sem.at[i]
-        )
-        for i in range(UP_CHUNKS)
-    ]
-    down_load = pltpu.make_async_copy(down, down_v, load_sem.at[UP_CHUNKS])
-    kv_local = mine * heads_dev // group - z * kv_heads_tp
-    kv_columns = pl.ds(pl.multiple_of(kv_local * 2 * HD, 2 * HD), 2 * HD)
-    kv_load = pltpu.make_async_copy(wkv.at[:, kv_columns], wkv_v, load_sem.at[UP_CHUNKS + 1])
-    q_load = pltpu.make_async_copy(wq, wq_v, load_sem.at[UP_CHUNKS + 2])
-    own_text = pltpu.make_async_copy(text, full.at[mine], own_sem)
-    own_text.start()
-    for load in up_loads:
-        load.start()
-    down_load.start()
-    kv_load.start()
-    q_load.start()
-
     tensor_peers = []
     for step in range(1, members):
         other = lax.rem(mine + step, members)
@@ -281,6 +260,28 @@
     barrier = pltpu.get_barrier_semaphore()
     for _, where in tensor_peers + ctx_peers:
         pl.semaphore_signal(barrier, inc=1, device_id=where, device_id_type=MESH)
+
+    span = vgain.shape[0] * vgain.shape[1]
+    up_chunks = features_in // span
+    up_loads = [
+        pltpu.make_async_copy(
+            up.at[:, pl.ds(i * span, span)], up_v.at[:, pl.ds(i * span, span)], load_sem.at[i]
+        )
+        for i in range(up_chunks)
+    ]
+    down_load = pltpu.make_async_copy(down, down_v, load_sem.at[up_chunks])
+    kv_local = mine * heads_dev // group - z * kv_heads_tp
+    kv_columns = pl.ds(pl.multiple_of(kv_local * 2 * HD, 2 * HD), 2 * HD)
+    kv_load = pltpu.make_async_copy(wkv.at[:, kv_columns], wkv_v, load_sem.at[up_chunks + 1])
+    q_load = pltpu.make_async_copy(wq, wq_v, load_sem.at[up_chunks + 2])
+    own_text = pltpu.make_async_copy(text, full.at[mine], own_sem)
+    own_text.start()
+    for load in up_loads:
+        load.start()
+    down_load.start()
+    kv_load.start()
+    q_load.start()
+
     pl.semaphore_wait(barrier, len(tensor_peers) + len(ctx_peers))
 
     def up_copy(step):
@@ -341,18 +342,20 @@
 
     text_step(0)
 
-    grouped = patches.shape[1] // vgain.shape[1]
-    span = vgain.shape[1]
+    gain = jnp.concatenate([vgain[i : i + 1, :] for i in range(vgain.shape[0])], axis=1)
     normed = []
-    for i in range(grouped):
+    for i in range(up_chunks):
         piece = patches[:, i * span : (i + 1) * span].astype(F32)
         scale = lax.rsqrt(jnp.mean(piece * piece, axis=-1, keepdims=True) + EPSILON)
-        normed.append((piece * scale * vgain[...]).astype(BF16))
-    hidden = jnp.zeros((rows, up.shape[1]), F32)
-    for i in range(UP_CHUNKS):
+        normed.append((piece * scale * gain).astype(BF16))
+    hidden = jnp.zeros((rows, up.shape[0]), F32)
+    for i in range(up_chunks):
         up_loads[i].wait()
-        hidden = hidden + jnp.dot(
-            normed[i], up_v[i * part : (i + 1) * part, :], preferred_element_type=F32
+        hidden = hidden + lax.dot_general(
+            normed[i],
+            up_v[:, i * span : (i + 1) * span],
+            (((1,), (1,)), ((), ())),
+            preferred_element_type=F32,
         )
     hidden = (0.5 * hidden * (1.0 + erf(hidden * 0.5**0.5))).astype(BF16)
     down_load.wait()
@@ -563,7 +566,7 @@
     kernel = functools.partial(body, ctx_size, tp_size, grp_size, KVH // tp_size)
     return pl.pallas_call(
         kernel,
-        out_shape=jax.ShapeDtypeStruct((tokens_dev, query_weight.shape[1]), BF16),
+        out_shape=pltpu.VMEM((tokens_dev, query_weight.shape[1]), BF16),
         in_specs=[
             vmem,
             scalars,
@@ -578,7 +581,7 @@
         ],
         out_specs=vmem,
         scratch_shapes=[
-            pltpu.VMEM(merge_up.shape, BF16),
+            pltpu.VMEM(merge_up.shape[::-1], BF16),
             pltpu.VMEM(merge_down.shape, BF16),
             pltpu.VMEM(query_weight.shape, BF16),
             pltpu.VMEM((features, 2 * HD), BF16),
@@ -592,7 +595,7 @@
             pltpu.VMEM((tokens_dev, features), BF16),
             pltpu.VMEM((tokens_dev, query_weight.shape[1]), BF16),
             pltpu.VMEM((ctx_size, tokens_dev, 2 * HD), BF16),
-            dma((UP_CHUNKS + 3,)),
+            dma((patches.shape[1] // vision_gain.shape[0] + 3,)),
             dma,
             dma((members,)),
             dma((tp_size,)),
@@ -617,8 +620,8 @@
         route_count,
         text_states,
         segment_ids.reshape(ctx_size, tokens_dev),
-        vision_gain.reshape(1, -1),
-        merge_up,
+        vision_gain.reshape(-1, HD),
+        merge_up.T,
         merge_down,
         norm_gain.reshape(1, -1),
         query_weight,

time: 39.8 us -> 31.1 us (0.78)
  local copies, waits for them, and re-layouts: 8.71 us -> 0.66 us
  Pallas kernels: 30.8 us -> 30.3 us
    unnamed x2 -> x1, local copies, waits for them, and re-layouts: 7.41 us -> 0.66 us
    reshape x1 -> x0, local copies, waits for them, and re-layouts: 1.29 us -> none  [fused(): vision_gain.reshape(1, -1)]
    pallas_call x1, Pallas kernels: 30.8 us -> 30.3 us  [fused(): pl.pallas_call(kernel, out_shape=pltpu.VMEM((tokens_dev, query_weight.sha...]
where the time goes in v2:
time: 31.1 us; the launch traced here: 30.9 us
  Pallas kernels  30.3 us (97%)
  local copies, waits for them, and re-layouts  0.66 us (2%)
    pallas_call x1, Pallas kernels, fused(): pl.pallas_call(kernel, out_shape=pltpu.VMEM((tokens_dev, query_weight.sha...  30.3 us
    unnamed x1, local copies, waits for them, and re-layouts  0.66 us

profile of v2, /device:TPU:0, one launch (start us, length us, event | category | flops | bytes accessed | tf_op | source)
XLA Modules:
  0.0 30.9 jit_solution(13929907742702915453)
XLA Ops:
  0.0 30.3 %shard_map.100 = bf16[128,512]{1,0:T(8,128)(2,1)S(1)} custom-call(bf16[8,5120]{1,0:T(8,128)(2,1)} %patches.1, s32[4,4]{1,0:T(4,128)} %route.1, bf16[128,512]{1,0:T(8,128)(2,1)} %text.1, s32[4,128]{1,0:T(4,128)} %bitcast.7, f32[10,128]{1,0:T(8,128)} %bitcast.6, bf16[320,5120]{1,0:T(8,128)(2,1)} %bitcast.4, bf16[320,4096]{1,0:T(8,128)(2,1)} %down.1, ...), custom_call_target="tpu_custom_call" | custom-call | tf_op jit(solution)/shard_map/pallas_call | solution.py:567
  30.3 0.7 %copy.12 = bf16[128,512]{1,0:T(8,128)(2,1)} copy(bf16[128,512]{1,0:T(8,128)(2,1)S(1)} %shard_map.100) | data formatting | bytes 262144

commit v3 on v2

--- a/solution.py
+++ b/solution.py
@@ -149,10 +149,11 @@
 MESH = pl.DeviceIdType.MESH
 BF16 = jnp.bfloat16
 F32 = jnp.float32
+HALVES = 2
 
 
 def fits(mesh):
-    return mesh.shape["grp"] == 2 and mesh.size <= 64
+    return mesh.shape["grp"] == 2 and mesh.shape["tp"] > 2 and mesh.size <= 64
 
 
 def erf(value):
@@ -216,8 +217,10 @@
     merged,
     arrived,
     gathered,
-    vis,
-    normal,
+    vis_mine,
+    vis_send_rows,
+    kv_sum,
+    q_sum,
     queries,
     kv_full,
     load_sem,
@@ -233,7 +236,6 @@
     row_own,
     vis_send,
     vis_recv,
-    vis_own,
     kv_send,
     kv_recv,
 ):
@@ -281,66 +283,6 @@
     down_load.start()
     kv_load.start()
     q_load.start()
-
-    pl.semaphore_wait(barrier, len(tensor_peers) + len(ctx_peers))
-
-    def up_copy(step):
-        slot = (z - step) * grp_size + g
-        src = text if step == 0 else full.at[slot]
-        return remote(src, full.at[slot], up_send.at[step], text_recv.at[slot], {"tp": z + 1})
-
-    def down_copy(step):
-        slot = (z + step) * grp_size + g
-        src = text if step == 0 else full.at[slot]
-        return remote(src, full.at[slot], down_send.at[step], text_recv.at[slot], {"tp": z - 1})
-
-    def side_copy(from_z, own):
-        slot = from_z * grp_size + g
-        src = text if own else full.at[slot]
-        return remote(src, full.at[slot], side_send.at[from_z], text_recv.at[slot], {"grp": 1 - g})
-
-    def slot_arrived(slot):
-        remote(
-            full.at[slot], full.at[slot], up_send.at[0], text_recv.at[slot], {"grp": 1 - g}
-        ).wait_recv()
-
-    def sends_up(step):
-        return (z >= step) & (z + 1 < tp_size)
-
-    def sends_down(step):
-        return (z + step < tp_size) & (z >= 1)
-
-    def text_step(step):
-        if step == 0:
-            side_now = [(z, None)]
-        else:
-            side_now = [(z - step, z >= step), (z + step, z + step < tp_size)]
-            for from_z, there in side_now:
-
-                @pl.when(there)
-                def _():
-                    slot_arrived(from_z * grp_size + g)
-
-        if step < tp_size - 1:
-
-            @pl.when(sends_up(step))
-            def _():
-                up_copy(step).start()
-
-            @pl.when(sends_down(step))
-            def _():
-                down_copy(step).start()
-
-        for from_z, there in side_now:
-            if there is None:
-                side_copy(from_z, True).start()
-            else:
-
-                @pl.when(there)
-                def _():
-                    side_copy(from_z, False).start()
-
-    text_step(0)
 
     gain = jnp.concatenate([vgain[i : i + 1, :] for i in range(vgain.shape[0])], axis=1)
     normed = []
@@ -365,6 +307,106 @@
         )
         rs_send[t] = piece.astype(rs_send.dtype)
 
+    pl.semaphore_wait(barrier, len(tensor_peers) + len(ctx_peers))
+
+    half_rows = tokens_dev // HALVES
+
+    def part_of(half):
+        return pl.ds(half * half_rows, half_rows)
+
+    def text_copy(slot, half, own, send, where):
+        src = text if own else full.at[slot]
+        return remote(
+            src.at[part_of(half)],
+            full.at[slot, part_of(half)],
+            send,
+            text_recv.at[slot, half],
+            where,
+        )
+
+    def up_copy(step, half):
+        slot = (z - step) * grp_size + g
+        return text_copy(slot, half, step == 0, up_send.at[step, half], {"tp": z + 1})
+
+    def down_copy(step, half):
+        slot = (z + step) * grp_size + g
+        return text_copy(slot, half, step == 0, down_send.at[step, half], {"tp": z - 1})
+
+    def side_copy(from_z, half, own):
+        slot = from_z * grp_size + g
+        return text_copy(slot, half, own, side_send.at[from_z, half], {"grp": 1 - g})
+
+    def slot_arrived(slot, half):
+        text_copy(slot, half, False, up_send.at[0, half], {"grp": 1 - g}).wait_recv()
+
+    def sends_up(step):
+        return (z >= step) & (z + 1 < tp_size)
+
+    def sends_down(step):
+        return (z + step < tp_size) & (z >= 1)
+
+    def text_step(step, half):
+        def forward():
+            if step < tp_size - 1:
+
+                @pl.when(sends_up(step))
+                def _():
+                    up_copy(step, half).start()
+
+                @pl.when(sends_down(step))
+                def _():
+                    down_copy(step, half).start()
+
+        if step == 0:
+            forward()
+            side_copy(z, half, True).start()
+            return
+        arriving = [(z - step, z >= step), (z + step, z + step < tp_size)]
+        for from_z, there in arriving:
+
+            @pl.when(there)
+            def _():
+                slot_arrived(from_z * grp_size + g, half)
+
+        forward()
+        for from_z, there in arriving:
+
+            @pl.when(there)
+            def _():
+                side_copy(from_z, half, False).start()
+
+    def nearest(k):
+        found = jnp.int32(0)
+        for at in range(tp_size):
+            order = sorted(range(tp_size), key=lambda other: (abs(other - at), other))
+            found = found + (z == at).astype(jnp.int32) * order[k]
+        return found
+
+    def gained(slot, at=pl.ds(0, tokens_dev)):
+        columns = pl.ds(pl.multiple_of(slot * width, width), width)
+        piece = full[slot, at].astype(F32)
+        square = jnp.sum(piece * piece, axis=-1, keepdims=True)
+        return (piece * ngain[:, columns]).astype(BF16), square, columns
+
+    def project(piece, columns, weight):
+        return jnp.dot(piece, weight[columns, :], preferred_element_type=F32)
+
+    def side_slot(k):
+        slot = nearest(k) * grp_size + 1 - g
+        for half in range(HALVES):
+            slot_arrived(slot, half)
+        return slot
+
+    def take(slot, squares):
+        piece, square, columns = gained(slot)
+        if squares is None:
+            kv_sum[...] = project(piece, columns, wkv_v)
+            q_sum[...] = project(piece, columns, wq_v)
+            return square
+        kv_sum[...] += project(piece, columns, wkv_v)
+        q_sum[...] += project(piece, columns, wq_v)
+        return squares + square
+
     rs_copies = []
     for i, (other, where) in enumerate(tensor_peers):
         copy = remote(
@@ -372,83 +414,9 @@
         )
         copy.start()
         rs_copies.append(copy)
-    for step in range(1, tp_size - 1):
-        text_step(step)
-    total = rs_send[mine].astype(F32)
-    for i, (other, where) in enumerate(tensor_peers):
-        remote(
-            rs_send.at[other], rs_recv.at[other], rs_send_sem.at[i], rs_recv_sem.at[other], where
-        ).wait_recv()
-        total = total + rs_recv[other].astype(F32)
-    total = total.astype(BF16).astype(merged.dtype)
-    for d in range(ctx_size):
-        merged[d] = total[d * bucket : (d + 1) * bucket, :]
-
-    row_copies = []
-    for i, (other, where) in enumerate(ctx_peers):
-        copy = remote(
-            merged.at[other], arrived.at[c], row_send.at[i], row_recv.at[c], where
-        )
-        copy.start()
-        row_copies.append(copy)
-    row_keep = pltpu.make_async_copy(merged.at[c], arrived.at[c], row_own)
-    row_keep.start()
-    text_step(tp_size - 1)
-    row_keep.wait()
-    for i, (other, where) in enumerate(ctx_peers):
-        remote(
-            merged.at[other], arrived.at[other], row_send.at[i], row_recv.at[other], where
-        ).wait_recv()
-    vis_copies = []
-    for i, (other, where) in enumerate(tensor_peers):
-        copy = remote(arrived, gathered.at[mine], vis_send.at[i], vis_recv.at[mine], where)
-        copy.start()
-        vis_copies.append(copy)
-    vis_keep = pltpu.make_async_copy(arrived, gathered.at[mine], vis_own)
-    vis_keep.start()
-
-    own_text.wait()
-    for t in range(members):
-
-        @pl.when(t % grp_size != g)
-        def _():
-            slot_arrived(t)
-
-    squares = jnp.zeros((tokens_dev, 1), F32)
-    for t in range(members):
-        piece = full[t].astype(F32)
-        squares = squares + jnp.sum(piece * piece, axis=-1, keepdims=True)
-    features = members * width
-    scale = lax.rsqrt(squares / features + EPSILON)
-    for t in range(members):
-        gain = ngain[:, t * width : (t + 1) * width]
-        normal[:, t * width : (t + 1) * width] = (full[t].astype(F32) * scale * gain).astype(BF16)
-    kv_load.wait()
-    kv_full[c] = jnp.dot(normal[...], wkv_v[...], preferred_element_type=F32).astype(BF16)
+    for half in range(HALVES):
+        text_step(0, half)
     late = -(-vis_rows // 16) * 16
-    tail = pl.ds(late, tokens_dev - late)
-    first = pl.ds(0, late)
-    kv_copies = []
-
-    def kv_copy(i, where, block, span_rows, phase):
-        return remote(
-            kv_full.at[block, span_rows],
-            kv_full.at[block, span_rows],
-            kv_send.at[phase, i],
-            kv_recv.at[phase, block],
-            where,
-        )
-
-    for i, (other, where) in enumerate(ctx_peers):
-        copy = kv_copy(i, where, c, tail, 0)
-        copy.start()
-        kv_copies.append(copy)
-    q_load.wait()
-    for n in range(0, queries.shape[1], 2 * HD):
-        queries[:, n : n + 2 * HD] = jnp.dot(
-            normal[...], wq_v[:, n : n + 2 * HD], preferred_element_type=F32
-        ).astype(BF16)
-
     slot_of = lax.broadcasted_iota(jnp.int32, (late, vis_rows), 0)
     row_of = lax.broadcasted_iota(jnp.int32, (late, vis_rows), 1)
     chosen = jnp.zeros((late, vis_rows), F32)
@@ -463,35 +431,110 @@
     chosen = chosen.astype(BF16)
     is_visual = lax.broadcasted_iota(jnp.int32, (late, 1), 0) < start
 
-    vis_keep.wait()
+    own_text.wait()
+    kv_load.wait()
+    q_load.wait()
+    squares = take(mine, None)
+    for half in range(HALVES):
+        text_step(1, half)
+    total = rs_send[mine].astype(F32)
     for i, (other, where) in enumerate(tensor_peers):
         remote(
-            arrived, gathered.at[other], vis_send.at[i], vis_recv.at[other], where
+            rs_send.at[other], rs_recv.at[other], rs_send_sem.at[i], rs_recv_sem.at[other], where
         ).wait_recv()
-    for t in range(members):
-        for source in range(ctx_size):
-            vis[source * bucket : (source + 1) * bucket, t * width : (t + 1) * width] = gathered[
-                t, source
-            ].astype(F32)
-    visual = vis[...]
-    scale = lax.rsqrt(jnp.mean(visual * visual, axis=-1, keepdims=True) + EPSILON)
-    visual = (visual * scale * ngain[...]).astype(BF16)
-    visual = jnp.dot(chosen, visual, preferred_element_type=F32).astype(BF16)
-    kv_rows = jnp.dot(visual, wkv_v[...], preferred_element_type=F32).astype(BF16)
-    kv_full[c, 0:late, :] = jnp.where(
-        is_visual, kv_rows.astype(F32), kv_full[c, 0:late, :].astype(F32)
-    ).astype(BF16)
+        total = total + rs_recv[other].astype(F32)
+    total = total.astype(BF16).astype(merged.dtype)
+    for d in range(ctx_size):
+        merged[d] = total[d * bucket : (d + 1) * bucket, :]
+
+    row_copies = []
     for i, (other, where) in enumerate(ctx_peers):
-        copy = kv_copy(i, where, c, first, 1)
+        copy = remote(
+            merged.at[other], arrived.at[c], row_send.at[i], row_recv.at[c], where
+        )
         copy.start()
-        kv_copies.append(copy)
-    for n in range(0, queries.shape[1], 2 * HD):
-        query_rows = jnp.dot(visual, wq_v[:, n : n + 2 * HD], preferred_element_type=F32)
-        queries[0:late, n : n + 2 * HD] = jnp.where(
-            is_visual,
-            query_rows.astype(BF16).astype(F32),
-            queries[0:late, n : n + 2 * HD].astype(F32),
-        ).astype(BF16)
+        row_copies.append(copy)
+    row_keep = pltpu.make_async_copy(merged.at[c], arrived.at[c], row_own)
+    row_keep.start()
+    squares = take(side_slot(0), squares)
+    for step in range(2, tp_size - 1):
+        text_step(step, 0)
+        squares = take(nearest(step - 1) * grp_size + g, squares)
+        for half in range(1, HALVES):
+            text_step(step, half)
+        squares = take(side_slot(step - 1), squares)
+    row_keep.wait()
+    for i, (other, where) in enumerate(ctx_peers):
+        remote(
+            merged.at[other], arrived.at[other], row_send.at[i], row_recv.at[other], where
+        ).wait_recv()
+    for source in range(ctx_size):
+        vis_mine[source * bucket : (source + 1) * bucket, :] = arrived[source]
+    vis_send_rows[...] = vis_mine[...].astype(BF16)
+    vis_copies = []
+
+    def vis_copy(slot, sem, own, where):
+        src = vis_send_rows if own else gathered.at[slot]
+        return remote(src, gathered.at[slot], vis_send.at[sem], vis_recv.at[slot], where)
+
+    line_peers = [lax.rem(z + step, tp_size) for step in range(1, tp_size)]
+    for i, other in enumerate(line_peers):
+        vis_copies.append(vis_copy(mine, i, True, {"tp": other}))
+    vis_copies.append(vis_copy(mine, tp_size - 1, True, {"grp": 1 - g}))
+    for copy in vis_copies:
+        copy.start()
+
+    def share_visual():
+        for i, other in enumerate(line_peers):
+            slot = other * grp_size + g
+            vis_copy(slot, i, False, {"tp": other}).wait_recv()
+            copy = vis_copy(slot, tp_size + i, False, {"grp": 1 - g})
+            copy.start()
+            vis_copies.append(copy)
+
+    gathered[mine] = vis_send_rows[...]
+    squares = take(nearest(tp_size - 2) * grp_size + g, squares)
+    squares = take(side_slot(tp_size - 2), squares)
+
+    near_slot = nearest(tp_size - 1) * grp_size + g
+    far_slot = nearest(tp_size - 1) * grp_size + 1 - g
+
+    def kv_copy(i, where, block, half):
+        if half == 0:
+            span_rows = pl.ds(late, half_rows - late)
+        elif half == HALVES:
+            span_rows = pl.ds(0, late)
+        else:
+            span_rows = part_of(half)
+        return remote(
+            kv_full.at[block, span_rows],
+            kv_full.at[block, span_rows],
+            kv_send.at[i, half],
+            kv_recv.at[block, half],
+            where,
+        )
+
+    kv_copies = []
+    for half in range(HALVES):
+        text_step(tp_size - 1, half)
+        at = part_of(half)
+        near_piece, near_square, near_columns = gained(near_slot, at)
+        kv_now = kv_sum[at, :] + project(near_piece, near_columns, wkv_v)
+        slot_arrived(far_slot, half)
+        far_piece, far_square, far_columns = gained(far_slot, at)
+        square = squares[half * half_rows : (half + 1) * half_rows] + near_square + far_square
+        scale = lax.rsqrt(square / (members * width) + EPSILON)
+        kv_now = (kv_now + project(far_piece, far_columns, wkv_v)) * scale
+        kv_full[c, at, :] = kv_now.astype(BF16)
+        for i, (other, where) in enumerate(ctx_peers):
+            copy = kv_copy(i, where, c, half)
+            copy.start()
+            kv_copies.append(copy)
+        q_now = q_sum[at, :] + project(near_piece, near_columns, wq_v)
+        q_now = (q_now + project(far_piece, far_columns, wq_v)) * scale
+        queries[at, :] = q_now.astype(BF16)
+        if half == 0:
+            share_visual()
 
     mine_row = jnp.broadcast_to(seg[pl.ds(c, 1), :], (tokens_dev, tokens_dev))
     query_seg = mine_row.T
@@ -507,9 +550,28 @@
         allowed.append((query_seg == seg[block : block + 1, :]) & near)
     bias = jnp.concatenate([jnp.where(ok, 0.0, NEGATIVE) for ok in allowed], axis=1)
 
-    for phase, span_rows in ((0, tail), (1, first)):
-        for i, (other, where) in enumerate(ctx_peers):
-            kv_copy(i, where, other, span_rows, phase).wait_recv()
+    for other in range(tp_size):
+        vis_copy(other * grp_size + 1 - g, 0, False, {"grp": 1 - g}).wait_recv()
+    visual = jnp.concatenate([gathered[t].astype(F32) for t in range(members)], axis=1)
+    scale = lax.rsqrt(jnp.mean(visual * visual, axis=-1, keepdims=True) + EPSILON)
+    visual = (visual * scale * ngain[...]).astype(BF16)
+    visual = jnp.dot(chosen, visual, preferred_element_type=F32).astype(BF16)
+    kv_rows = jnp.dot(visual, wkv_v[...], preferred_element_type=F32)
+    kv_full[c, 0:late, :] = jnp.where(
+        is_visual, kv_rows, kv_full[c, 0:late, :].astype(F32)
+    ).astype(BF16)
+    for i, (other, where) in enumerate(ctx_peers):
+        copy = kv_copy(i, where, c, HALVES)
+        copy.start()
+        kv_copies.append(copy)
+    query_rows = jnp.dot(visual, wq_v[...], preferred_element_type=F32)
+    queries[0:late, :] = jnp.where(
+        is_visual, query_rows, queries[0:late, :].astype(F32)
+    ).astype(BF16)
+
+    for i, (other, where) in enumerate(ctx_peers):
+        for half in range(HALVES + 1):
+            kv_copy(i, where, other, half).wait_recv()
     keys = jnp.concatenate([kv_full[b, :, :HD] for b in range(ctx_size)], axis=0)
     values = jnp.concatenate([kv_full[b, :, HD:] for b in range(ctx_size)], axis=0)
     for h in range(heads_dev):
@@ -523,18 +585,19 @@
         mixed = jnp.dot(weights.astype(BF16), values, preferred_element_type=F32)
         out[:, h * HD : (h + 1) * HD] = (mixed / total).astype(BF16)
 
-    for step in range(tp_size - 1):
-
-        @pl.when(sends_up(step))
-        def _():
-            up_copy(step).wait_send()
-
-        @pl.when(sends_down(step))
-        def _():
-            down_copy(step).wait_send()
-
-    for from_z in range(tp_size):
-        side_copy(from_z, False).wait_send()
+    for half in range(HALVES):
+        for step in range(tp_size - 1):
+
+            @pl.when(sends_up(step))
+            def _():
+                up_copy(step, half).wait_send()
+
+            @pl.when(sends_down(step))
+            def _():
+                down_copy(step, half).wait_send()
+
+        for from_z in range(tp_size):
+            side_copy(from_z, half, False).wait_send()
     for copy in rs_copies + row_copies + vis_copies + kv_copies:
         copy.wait_send()
 
@@ -590,17 +653,19 @@
             pltpu.VMEM((members, rows, width), BF16),
             pltpu.VMEM((ctx_size, bucket, width), F32),
             pltpu.VMEM((ctx_size, bucket, width), F32),
-            pltpu.VMEM((members, ctx_size, bucket, width), F32),
-            pltpu.VMEM((rows, features), F32),
-            pltpu.VMEM((tokens_dev, features), BF16),
+            pltpu.VMEM((members, rows, width), BF16),
+            pltpu.VMEM((rows, width), F32),
+            pltpu.VMEM((rows, width), BF16),
+            pltpu.VMEM((tokens_dev, 2 * HD), F32),
+            pltpu.VMEM((tokens_dev, query_weight.shape[1]), F32),
             pltpu.VMEM((tokens_dev, query_weight.shape[1]), BF16),
             pltpu.VMEM((ctx_size, tokens_dev, 2 * HD), BF16),
             dma((patches.shape[1] // vision_gain.shape[0] + 3,)),
             dma,
-            dma((members,)),
-            dma((tp_size,)),
-            dma((tp_size,)),
-            dma((tp_size,)),
+            dma((members, HALVES)),
+            dma((tp_size, HALVES)),
+            dma((tp_size, HALVES)),
+            dma((tp_size, HALVES)),
             dma((members,)),
             dma((members,)),
             dma((ctx_size,)),
@@ -608,9 +673,8 @@
             dma,
             dma((members,)),
             dma((members,)),
-            dma,
-            dma((2, ctx_size)),
-            dma((2, ctx_size)),
+            dma((ctx_size, HALVES + 1)),
+            dma((ctx_size, HALVES + 1)),
         ],
         compiler_params=pltpu.CompilerParams(
             collective_id=0, has_side_effects=True, vmem_limit_bytes=56 * 2**20

time: 31.1 us -> 30.7 us (0.987)
  Pallas kernels: 30.3 us -> 29.9 us
    pallas_call x1, Pallas kernels: 30.3 us -> 29.9 us  [fused(): pl.pallas_call(kernel, out_shape=pltpu.VMEM((tokens_dev, query_weight.sha...]
where the time goes in v3:
time: 30.7 us; the launch traced here: 30.6 us
  Pallas kernels  29.9 us (97%)
  local copies, waits for them, and re-layouts  0.66 us (2%)
    pallas_call x1, Pallas kernels, fused(): pl.pallas_call(kernel, out_shape=pltpu.VMEM((tokens_dev, query_weight.sha...  29.9 us
    unnamed x1, local copies, waits for them, and re-layouts  0.66 us

profile of v3, /device:TPU:0, one launch (start us, length us, event | category | flops | bytes accessed | tf_op | source)
XLA Modules:
  0.0 30.6 jit_solution(15398591127964804676)
XLA Ops:
  0.0 29.9 %shard_map.100 = bf16[128,512]{1,0:T(8,128)(2,1)S(1)} custom-call(bf16[8,5120]{1,0:T(8,128)(2,1)} %patches.1, s32[4,4]{1,0:T(4,128)} %route.1, bf16[128,512]{1,0:T(8,128)(2,1)} %text.1, s32[4,128]{1,0:T(4,128)} %bitcast.7, f32[10,128]{1,0:T(8,128)} %bitcast.6, bf16[320,5120]{1,0:T(8,128)(2,1)} %bitcast.4, bf16[320,4096]{1,0:T(8,128)(2,1)} %down.1, ...), custom_call_target="tpu_custom_call" | custom-call | tf_op jit(solution)/shard_map/pallas_call | solution.py:630
  29.9 0.7 %copy.12 = bf16[128,512]{1,0:T(8,128)(2,1)} copy(bf16[128,512]{1,0:T(8,128)(2,1)S(1)} %shard_map.100) | data formatting | bytes 262144
